TPU v7x, 256 devices: a whole 4x4x8 slice. The times are simulated.
256 devices in a mesh: feat: 32 (over y, z), dp: 8 (over x, core).
Axes of the slice: x: 4, y: 4, z: 8, core: 2. Of those that a mesh axis runs over, the one named last changes fastest.
Arguments:
- face_grid: bfloat16 [32768, 10240], P('dp', 'feat'), may hold values from -6 to 6
- first_nbrs: int32 [16384, 8], P('dp'), may hold values from 0 to 4095
- first_count: int32 [16384], P('dp'), may hold values from 1 to 8
- w_first: bfloat16 [10240, 256], P('feat'), may hold values from -0.0625 to 0.0625
- b_first: float32 [256], replicated, may hold values from -3 to 3
- send_rows: int32 [4096], P('dp'), may hold values from 0 to 2047
- second_nbrs: int32 [16384, 8], P(('dp', 'feat')), may hold values from 0 to 2559
- second_count: int32 [16384], P(('dp', 'feat')), may hold values from 1 to 8
- w_in: bfloat16 [256, 1024], replicated, may hold values from -0.375 to 0.375
- w_out: bfloat16 [1024, 256], replicated, may hold values from -0.1875 to 0.1875
- out_grad: bfloat16 [16384, 256], P(('dp', 'feat')), may hold values from -6 to 6
Outputs:
- embed: bfloat16 [16384, 256], P(('dp', 'feat'))
- grad_first: float32 [10240, 256], P('feat')
Inputs may be any that keep to these rules, and one draw needn't show every extreme that they name: `first_count`: slots at or past a target's count are ignored; counts lie in 1 to 8. `first_nbrs`: only slots below first_count are read. `second_count`: slots at or past a target's count are ignored. `second_nbrs`: indices below 2048 name the partition's own targets, the rest the faces received from the previous partition in order; only slots below second_count are read. `send_rows`: entries may repeat.
All inputs are finite; a program needn't handle non-finite values.
Results may differ from a plain program's by a relative error of at most 0.0061.
Values may be sent and summed in bfloat16 or wider, within the bound.
No kernel may reach another device: no remote copies, remote signals or barrier semaphores. Data moves between devices by JAX's collectives and lax.ppermute only.
A program may use at most 64 MiB of HBM per device.

v0:
```python
import jax
import jax.numpy as jnp
from jax import lax
from jax.sharding import PartitionSpec as P


def passed_along(shard, axis, by):
    devices = lax.axis_size(axis)
    return lax.ppermute(shard, axis, [(i, (i + by) % devices) for i in range(devices)])


def slope(value):
    sig = jax.nn.sigmoid(value)
    return sig * (1.0 + value * (1.0 - sig))


def mean_rows(table, nbrs, count):
    total = jnp.zeros((nbrs.shape[0], table.shape[1]), jnp.float32)
    for slot in range(nbrs.shape[1]):
        picked = table[nbrs[:, slot]].astype(jnp.float32)
        total = total + jnp.where((slot < count)[:, None], picked, 0.0)
    return total / count[:, None].astype(jnp.float32)


def spread(grad, nbrs, count, size):
    slots = jnp.arange(nbrs.shape[1], dtype=jnp.int32)
    factor = jnp.where(
        slots[None, :] < count[:, None], 1.0 / count[:, None].astype(jnp.float32), 0.0
    )
    terms = (grad[:, None, :] * factor[:, :, None]).reshape(-1, grad.shape[1])
    return jax.ops.segment_sum(terms, nbrs.reshape(-1), num_segments=size)


def body(
    face_grid,
    first_nbrs,
    first_count,
    w_first,
    b_first,
    send_rows,
    second_nbrs,
    second_count,
    w_in,
    w_out,
    out_grad,
):
    targets = first_nbrs.shape[0]
    agg_first = (
        face_grid[:targets].astype(jnp.float32) + mean_rows(face_grid, first_nbrs, first_count)
    ).astype(jnp.bfloat16)
    partial_value = jnp.dot(agg_first, w_first, preferred_element_type=jnp.float32)
    pre_own = lax.psum_scatter(partial_value, "feat", scatter_dimension=0, tiled=True) + b_first
    hidden_own = jax.nn.silu(pre_own).astype(jnp.bfloat16)
    table = lax.all_gather(hidden_own, "feat", axis=0, tiled=True)
    received = passed_along(table[send_rows], "dp", 1)
    extended = jnp.concatenate([table, received], axis=0)
    agg_second = (
        hidden_own.astype(jnp.float32) + mean_rows(extended, second_nbrs, second_count)
    ).astype(jnp.bfloat16)
    pre_mlp = jnp.dot(agg_second, w_in, preferred_element_type=jnp.float32)
    act_mlp = jax.nn.silu(pre_mlp).astype(jnp.bfloat16)
    embed = (
        hidden_own.astype(jnp.float32) + jnp.dot(act_mlp, w_out, preferred_element_type=jnp.float32)
    ).astype(jnp.bfloat16)
    grad_act = lax.dot_general(
        out_grad, w_out, (((1,), (1,)), ((), ())), preferred_element_type=jnp.float32
    )
    grad_pre_mlp = (grad_act * slope(pre_mlp)).astype(jnp.bfloat16)
    grad_agg = lax.dot_general(
        grad_pre_mlp, w_in, (((1,), (1,)), ((), ())), preferred_element_type=jnp.float32
    )
    grad_ext = spread(grad_agg, second_nbrs, second_count, extended.shape[0])
    full_rows = table.shape[0]
    returned = passed_along(grad_ext[full_rows:].astype(jnp.bfloat16), "dp", -1).astype(jnp.float32)
    table_grad = grad_ext[:full_rows].at[send_rows].add(returned)
    own_terms = out_grad.astype(jnp.float32) + grad_agg
    grad_own = (
        lax.psum_scatter(
            table_grad.astype(jnp.bfloat16), "feat", scatter_dimension=0, tiled=True
        ).astype(jnp.float32)
        + own_terms
    )
    grad_pre_own = (grad_own * slope(pre_own)).astype(jnp.bfloat16)
    grad_pre_first = lax.all_gather(grad_pre_own, "feat", axis=0, tiled=True)
    slice_grad = lax.dot_general(
        agg_first, grad_pre_first, (((0,), (0,)), ((), ())), preferred_element_type=jnp.float32
    )
    grad_first = lax.psum(slice_grad, "dp")
    return (embed, grad_first)


def solution(mesh):
    return jax.shard_map(
        body,
        mesh=mesh,
        in_specs=(
            P("dp", "feat"),
            P("dp", None),
            P("dp"),
            P("feat", None),
            P(),
            P("dp"),
            P(("dp", "feat"), None),
            P(("dp", "feat")),
            P(),
            P(),
            P(("dp", "feat"), None),
        ),
        out_specs=(P(("dp", "feat"), None), P("feat", None)),
        check_vma=False,
    )
```

profile of v0, /device:TPU:8, one launch (start us, length us, event | category | flops | bytes accessed | tf_op | source)
XLA Modules:
  0.0 828.4 jit_solution(5859287706951482798)
XLA Ops:
  7.2 0.0 copy-start
  7.2 0.0 reduce-scatter.3.cloned.1.call-start
  7.2 0.8 broadcast_compare_fusion.7
  8.0 0.7 convert_element_type.107
  8.7 4.6 copy.22
  13.3 0.0 copy-done.5
  13.3 0.1 compare_select_fusion.7
  13.4 11.2 %gather_fusion = bf16[2048,320]{1,0:T(8,128)(2,1)} fusion(bf16[4096,320]{1,0:T(8,128)(2,1)} %copy.22, s32[2048]{0:T(1024)S(1)} %broadcast_clamp_fusion.7), kind=kCustom, calls=%fused_computation | custom fusion | bytes 2629632 | tf_op jit(solution)/shard_map/gather | solution.py:20
  24.6 11.2 %gather_fusion.1 = bf16[2048,320]{1,0:T(8,128)(2,1)} fusion(bf16[4096,320]{1,0:T(8,128)(2,1)} %copy.22, s32[2048]{0:T(1024)S(1)} %broadcast_clamp_fusion.6), kind=kCustom, calls=%fused_computation.1 | custom fusion | bytes 2629632 | tf_op jit(solution)/shard_map/gather | solution.py:20
  35.8 11.2 %gather_fusion.2 = bf16[2048,320]{1,0:T(8,128)(2,1)} fusion(bf16[4096,320]{1,0:T(8,128)(2,1)} %copy.22, s32[2048]{0:T(1024)S(1)} %broadcast_clamp_fusion.5), kind=kCustom, calls=%fused_computation.2 | custom fusion | bytes 2629632 | tf_op jit(solution)/shard_map/gather | solution.py:20
  47.0 11.2 %gather_fusion.3 = bf16[2048,320]{1,0:T(8,128)(2,1)} fusion(bf16[4096,320]{1,0:T(8,128)(2,1)} %copy.22, s32[2048]{0:T(1024)S(1)} %broadcast_clamp_fusion.4), kind=kCustom, calls=%fused_computation.3 | custom fusion | bytes 2629632 | tf_op jit(solution)/shard_map/gather | solution.py:20
  58.1 11.2 %gather_fusion.4 = bf16[2048,320]{1,0:T(8,128)(2,1)} fusion(bf16[4096,320]{1,0:T(8,128)(2,1)} %copy.22, s32[2048]{0:T(1024)S(1)} %broadcast_clamp_fusion.3), kind=kCustom, calls=%fused_computation.4 | custom fusion | bytes 2629632 | tf_op jit(solution)/shard_map/gather | solution.py:20
  69.3 11.2 %gather_fusion.5 = bf16[2048,320]{1,0:T(8,128)(2,1)} fusion(bf16[4096,320]{1,0:T(8,128)(2,1)} %copy.22, s32[2048]{0:T(1024)S(1)} %broadcast_clamp_fusion.2), kind=kCustom, calls=%fused_computation.5 | custom fusion | bytes 2629632 | tf_op jit(solution)/shard_map/gather | solution.py:20
  80.5 11.2 %gather_fusion.6 = bf16[2048,320]{1,0:T(8,128)(2,1)} fusion(bf16[4096,320]{1,0:T(8,128)(2,1)} %copy.22, s32[2048]{0:T(1024)S(1)} %broadcast_clamp_fusion.1), kind=kCustom, calls=%fused_computation.6 | custom fusion | bytes 2629632 | tf_op jit(solution)/shard_map/gather | solution.py:20
  91.7 11.2 %gather_fusion.7 = bf16[2048,320]{1,0:T(8,128)(2,1)} fusion(bf16[4096,320]{1,0:T(8,128)(2,1)} %copy.22, s32[2048]{0:T(1024)S(1)} %broadcast_clamp_fusion), kind=kCustom, calls=%fused_computation.7 | custom fusion | bytes 2629632 | tf_op jit(solution)/shard_map/gather | solution.py:20
  102.8 8.9 %add_convert_fusion = bf16[2048,320]{1,0:T(8,128)(2,1)S(1)} fusion(bf16[2048,320]{1,0:T(8,128)(2,1)} %gather_fusion.7, bf16[2048,320]{1,0:T(8,128)(2,1)} %gather_fusion.6, bf16[2048,320]{1,0:T(8,128)(2,1)} %gather_fusion.5, bf16[2048,320]{1,0:T(8,128)(2,1)} %gather_fusion.4, bf16[2048,320]{1,0:T(8,128)(2,1)} %gather_fusion.3, ...), kind=kLoop, calls=%fused_computation.19 | loop fusion | flops 17694720 | bytes 13131776 | tf_op jit(solution)/shard_map/convert_element_type | solution.py:50
  111.8 2.0 fusion.40
  113.8 0.0 reduce-scatter.3.cloned.1.call-update
  113.8 0.0 all-gather.3.cloned.1.call-start
  113.9 220.8 %reduce-scatter.3.cloned.1.call-done = f32[64,256]{1,0:T(8,128)} async-done(((f32[2048,256]{1,0:T(8,128)}), f32[64,256]{1,0:T(8,128)}) %reduce-scatter.3.cloned.1.call-update) | async-done | bytes 65552 | tf_op jit(solution)/shard_map/reduce_scatter | solution.py:52
  334.7 1.5 multiply_convert_fusion.3
  336.2 0.0 all-gather.3.cloned.1.call-update
  336.2 0.2 reduce-scatter.5.cloned.1.call-start
  336.6 0.1 fusion.28
  336.6 75.6 %all-gather.3.cloned.1.call-done = bf16[2048,256]{1,0:T(8,128)(2,1)} async-done(((bf16[64,256]{1,0:T(8,128)(2,1)}), bf16[2048,256]{1,0:T(8,128)(2,1)}) %all-gather.3.cloned.1.call-update) | async-done | bytes 1048592 | tf_op jit(solution)/shard_map/all_gather | solution.py:54
  412.2 3.6 gather_fusion.8
  415.9 0.0 collective-permute-start
  415.9 0.1 copy.31
  416.0 0.1 select_n.163
  416.1 0.1 reshape.203
  416.2 1.1 constant_dynamic-update-slice_fusion.1
  417.3 5.8 collective-permute-done
  423.1 0.7 constant_dynamic-update-slice_fusion
  423.8 2.1 gather_fusion.10
  426.0 0.0 copy-start.6
  426.0 0.0 copy-start.11
  426.0 2.2 gather_fusion.11
  428.2 2.1 gather_fusion.12
  430.3 2.1 gather_fusion.13
  432.5 2.1 gather_fusion.14
  434.6 2.1 gather_fusion.15
  436.8 2.1 gather_fusion.9
  438.9 2.1 gather_fusion.16
  441.1 0.3 fusion.16
  441.4 0.5 fusion.3
  441.9 5.1 scatter_custom_fusion
  447.0 1.1 slice.132
  448.0 0.0 collective-permute-start.1
  448.1 3.1 slice.112
  451.2 0.8 collective-permute-done.1
  451.9 6.0 scatter_custom_fusion.1
  457.9 2.7 convert_element_type.125
  460.6 0.0 reduce-scatter.5.cloned.1.call-update
  460.7 0.0 all-gather.5.cloned.1.call-start
  460.7 215.0 %reduce-scatter.5.cloned.1.call-done = bf16[64,256]{1,0:T(8,128)(2,1)} async-done(((bf16[2048,256]{1,0:T(8,128)(2,1)}), bf16[64,256]{1,0:T(8,128)(2,1)}) %reduce-scatter.5.cloned.1.call-update) | async-done | bytes 32784 | tf_op jit(solution)/shard_map/reduce_scatter | solution.py:78
  675.8 1.4 multiply_convert_fusion.2
  677.2 0.0 all-gather.5.cloned.1.call-update
  677.2 0.0 all-reduce.2.cloned.1.call-start
  677.2 75.9 %all-gather.5.cloned.1.call-done = bf16[2048,256]{1,0:T(8,128)(2,1)} async-done(((bf16[64,256]{1,0:T(8,128)(2,1)}), bf16[2048,256]{1,0:T(8,128)(2,1)}) %all-gather.5.cloned.1.call-update) | async-done | bytes 1048592 | tf_op jit(solution)/shard_map/all_gather | solution.py:84
  753.1 2.5 fusion.41
  755.7 0.0 all-reduce.2.cloned.1.call-update
  755.7 0.8 fusion.4
  756.6 63.6 %all-reduce.2.cloned.1.call-done = f32[320,256]{1,0:T(8,128)} async-done(((f32[320,256]{1,0:T(8,128)}), f32[320,256]{1,0:T(8,128)}) %all-reduce.2.cloned.1.call-update) | async-done | bytes 327696 | tf_op jit(solution)/shard_map/psum | solution.py:88
  820.1 1.7 copy.35
  (38 shorter events, 0.1 us)
Async XLA Ops:
  7.2 433.9 %copy-start = (bf16[256,1024]{1,0:T(8,128)(2,1)S(1)}, bf16[256,1024]{1,0:T(8,128)(2,1)}, u32[]{:S(2)}) copy-start(bf16[256,1024]{1,0:T(8,128)(2,1)} %param.19) | copy-start | bytes 1572868
  7.2 327.5 %reduce-scatter.3.cloned.1.call-start = ((), (), s32[]{:S(2)}) async-start(), calls=%async_computation.2 | async-start | bytes 2162688 | tf_op jit(solution)/shard_map/reduce_scatter | solution.py:52
  8.7 4.6 copy-start.5
  102.8 8.9 %copy-start.3 = (bf16[320,256]{1,0:T(8,128)(2,1)S(1)}, bf16[320,256]{1,0:T(8,128)(2,1)}, u32[]{:S(2)}) copy-start(bf16[320,256]{1,0:T(8,128)(2,1)} %param.14) | copy-start | bytes 491524
  113.8 220.9 %copy-start.8 = (f32[256]{0:T(256)S(1)}, f32[256]{0:T(256)}, u32[]{:S(2)}) copy-start(f32[256]{0:T(256)} %param.15) | copy-start | bytes 3076
  113.8 222.6 %copy-start.10 = (s32[512]{0:T(512)S(1)}, s32[512]{0:T(512)}, u32[]{:S(2)}) copy-start(s32[512]{0:T(512)} %param.16) | copy-start | bytes 6148
  113.8 222.7 %copy-start.7 = (s32[64,8]{0,1:T(8,128)S(1)}, s32[64,8]{0,1:T(8,128)}, u32[]{:S(2)}) copy-start(s32[64,8]{0,1:T(8,128)} %param.17) | copy-start | bytes 6148
  113.8 222.7 %copy-start.9 = (s32[64]{0:T(128)S(1)}, s32[64]{0:T(128)}, u32[]{:S(2)}) copy-start(s32[64]{0:T(128)} %param.18) | copy-start | bytes 772
  113.8 298.4 %all-gather.3.cloned.1.call-start = ((), (), s32[]{:S(2)}) async-start(), calls=%async_computation.3 | async-start | bytes 1081344 | tf_op jit(solution)/shard_map/all_gather | solution.py:54
  336.2 339.6 %reduce-scatter.5.cloned.1.call-start = ((), (), s32[]{:S(2)}) async-start(), calls=%async_computation.4 | async-start | bytes 1081344 | tf_op jit(solution)/shard_map/reduce_scatter | solution.py:78
  412.2 3.9 copy-start.1
  415.9 7.2 collective-permute-start
  417.3 23.8 %copy-start.4 = (bf16[64,256]{1,0:T(8,128)(2,1)S(1)}, bf16[64,256]{1,0:T(8,128)(2,1)}, u32[]{:S(2)}) copy-start(bf16[64,256]{1,0:T(8,128)(2,1)} %multiply_convert_fusion.3) | copy-start | bytes 98308
  426.0 15.4 %copy-start.6 = (bf16[64,256]{1,0:T(8,128)(2,1)S(1)}, bf16[64,256]{1,0:T(8,128)(2,1)}, u32[]{:S(2)}) copy-start(bf16[64,256]{1,0:T(8,128)(2,1)} %param.21) | copy-start | bytes 98308
  426.0 15.4 %copy-start.11 = (bf16[1024,256]{1,0:T(8,128)(2,1)S(1)}, bf16[1024,256]{1,0:T(8,128)(2,1)}, u32[]{:S(2)}) copy-start(bf16[1024,256]{1,0:T(8,128)(2,1)} %param.20) | copy-start | bytes 1572868
  448.0 3.9 collective-permute-start.1
  457.9 217.8 %copy-start.2 = (f32[64,256]{1,0:T(8,128)S(1)}, f32[64,256]{1,0:T(8,128)}, u32[]{:S(2)}) copy-start(f32[64,256]{1,0:T(8,128)} %reduce-scatter.3.cloned.1.call-done) | copy-start | bytes 196612
  460.7 292.5 %all-gather.5.cloned.1.call-start = ((), (), s32[]{:S(2)}) async-start(), calls=%async_computation.5 | async-start | bytes 1081344 | tf_op jit(solution)/shard_map/all_gather | solution.py:84
  677.2 142.9 %all-reduce.2.cloned.1.call-start = ((), (), s32[]{:S(2)}) async-start(), calls=%async_computation.6 | async-start | bytes 655360 | tf_op jit(solution)/shard_map/psum | solution.py:88
Sparse Core Ops, SparseCore 0:
  113.9 220.6 reduce-scatter.2
  337.8 74.3 all-gather.2
  460.8 214.9 reduce-scatter.4
  678.8 74.3 all-gather.4
  755.9 64.2 all-reduce.1
where the time goes:
time: 830 us; the launch traced here: 828 us
  waiting for transfers between devices  658 us (79%)
  local copies, waits for them, and re-layouts  123 us (15%)
  other arithmetic  27.3 us (3%)
  between operations  14 us (2%)
    reduce_scatter x1, waiting for transfers between devices, body(): lax.psum_scatter(partial_value, 'feat', scatter_dimension=0, tiled=True)  221 us
    reduce_scatter x1, waiting for transfers between devices, body(): lax.psum_scatter(table_grad.astype(jnp.bfloat16), 'feat', scatter_dimensi...  215 us
    gather x16, local copies, waits for them, and re-layouts, mean_rows(): picked = table[nbrs[:, slot]].astype(jnp.float32)  107 us
    all_gather x1, waiting for transfers between devices, body(): grad_pre_first = lax.all_gather(grad_pre_own, 'feat', axis=0, tiled=True)  75.9 us
    all_gather x1, waiting for transfers between devices, body(): table = lax.all_gather(hidden_own, 'feat', axis=0, tiled=True)  75.6 us
    psum x1, waiting for transfers between devices, body(): grad_first = lax.psum(slice_grad, 'dp')  63.6 us
  transfers between devices with their start and end apart: 7, of which 7 were waited for; matrix products, arithmetic and copies ran while one was open for 1% of the time, Pallas kernels for 0%

commit v1 on v0

--- a/solution.py
+++ b/solution.py
@@ -85,7 +85,7 @@
     slice_grad = lax.dot_general(
         agg_first, grad_pre_first, (((0,), (0,)), ((), ())), preferred_element_type=jnp.float32
     )
-    grad_first = lax.psum(slice_grad, "dp")
+    grad_first = jnp.sum(lax.all_gather(slice_grad, "dp"), axis=0)
     return (embed, grad_first)
 
 

time: 830 us -> 795 us (0.958)
  waiting for transfers between devices: 658 us -> 620 us
    psum x1 -> x0, waiting for transfers between devices: 63.6 us -> none  [body(): grad_first = lax.psum(slice_grad, 'dp')]
    all_gather x0 -> x1, waiting for transfers between devices: none -> 26.4 us  [body(): grad_first = jnp.sum(lax.all_gather(slice_grad, 'dp'), axis=0)]
where the time goes in v1:
time: 795 us; the launch traced here: 792 us
  waiting for transfers between devices  620 us (78%)
  local copies, waits for them, and re-layouts  121 us (15%)
  other arithmetic  29.9 us (4%)
  between operations  14 us (2%)
    reduce_scatter x1, waiting for transfers between devices, body(): lax.psum_scatter(partial_value, 'feat', scatter_dimension=0, tiled=True)  221 us
    reduce_scatter x1, waiting for transfers between devices, body(): lax.psum_scatter(table_grad.astype(jnp.bfloat16), 'feat', scatter_dimensi...  215 us
    gather x16, local copies, waits for them, and re-layouts, mean_rows(): picked = table[nbrs[:, slot]].astype(jnp.float32)  107 us
    all_gather x1, waiting for transfers between devices, body(): grad_pre_first = lax.all_gather(grad_pre_own, 'feat', axis=0, tiled=True)  75.9 us
    all_gather x1, waiting for transfers between devices, body(): table = lax.all_gather(hidden_own, 'feat', axis=0, tiled=True)  75.6 us
    all_gather x1, waiting for transfers between devices, body(): grad_first = jnp.sum(lax.all_gather(slice_grad, 'dp'), axis=0)  26.4 us
  transfers between devices with their start and end apart: 7, of which 7 were waited for; matrix products, arithmetic and copies ran while one was open for 1% of the time, Pallas kernels for 0%

profile of v1, /device:TPU:8, one launch (start us, length us, event | category | flops | bytes accessed | tf_op | source)
XLA Modules:
  0.0 792.2 jit_solution(18360806083179991006)
XLA Ops:
  7.2 0.0 copy-start
  7.2 0.0 reduce-scatter.3.cloned.1.call-start
  7.2 0.8 broadcast_compare_fusion.7
  8.0 0.7 convert_element_type.107
  8.7 4.6 copy.22
  13.3 0.0 copy-done.5
  13.3 0.1 compare_select_fusion.7
  13.4 11.2 %gather_fusion = bf16[2048,320]{1,0:T(8,128)(2,1)} fusion(bf16[4096,320]{1,0:T(8,128)(2,1)} %copy.22, s32[2048]{0:T(1024)S(1)} %broadcast_clamp_fusion.7), kind=kCustom, calls=%fused_computation | custom fusion | bytes 2629632 | tf_op jit(solution)/shard_map/gather | solution.py:20
  24.6 11.2 %gather_fusion.1 = bf16[2048,320]{1,0:T(8,128)(2,1)} fusion(bf16[4096,320]{1,0:T(8,128)(2,1)} %copy.22, s32[2048]{0:T(1024)S(1)} %broadcast_clamp_fusion.6), kind=kCustom, calls=%fused_computation.1 | custom fusion | bytes 2629632 | tf_op jit(solution)/shard_map/gather | solution.py:20
  35.8 11.2 %gather_fusion.2 = bf16[2048,320]{1,0:T(8,128)(2,1)} fusion(bf16[4096,320]{1,0:T(8,128)(2,1)} %copy.22, s32[2048]{0:T(1024)S(1)} %broadcast_clamp_fusion.5), kind=kCustom, calls=%fused_computation.2 | custom fusion | bytes 2629632 | tf_op jit(solution)/shard_map/gather | solution.py:20
  47.0 11.2 %gather_fusion.3 = bf16[2048,320]{1,0:T(8,128)(2,1)} fusion(bf16[4096,320]{1,0:T(8,128)(2,1)} %copy.22, s32[2048]{0:T(1024)S(1)} %broadcast_clamp_fusion.4), kind=kCustom, calls=%fused_computation.3 | custom fusion | bytes 2629632 | tf_op jit(solution)/shard_map/gather | solution.py:20
  58.1 11.2 %gather_fusion.4 = bf16[2048,320]{1,0:T(8,128)(2,1)} fusion(bf16[4096,320]{1,0:T(8,128)(2,1)} %copy.22, s32[2048]{0:T(1024)S(1)} %broadcast_clamp_fusion.3), kind=kCustom, calls=%fused_computation.4 | custom fusion | bytes 2629632 | tf_op jit(solution)/shard_map/gather | solution.py:20
  69.3 11.2 %gather_fusion.5 = bf16[2048,320]{1,0:T(8,128)(2,1)} fusion(bf16[4096,320]{1,0:T(8,128)(2,1)} %copy.22, s32[2048]{0:T(1024)S(1)} %broadcast_clamp_fusion.2), kind=kCustom, calls=%fused_computation.5 | custom fusion | bytes 2629632 | tf_op jit(solution)/shard_map/gather | solution.py:20
  80.5 11.2 %gather_fusion.6 = bf16[2048,320]{1,0:T(8,128)(2,1)} fusion(bf16[4096,320]{1,0:T(8,128)(2,1)} %copy.22, s32[2048]{0:T(1024)S(1)} %broadcast_clamp_fusion.1), kind=kCustom, calls=%fused_computation.6 | custom fusion | bytes 2629632 | tf_op jit(solution)/shard_map/gather | solution.py:20
  91.7 11.2 %gather_fusion.7 = bf16[2048,320]{1,0:T(8,128)(2,1)} fusion(bf16[4096,320]{1,0:T(8,128)(2,1)} %copy.22, s32[2048]{0:T(1024)S(1)} %broadcast_clamp_fusion), kind=kCustom, calls=%fused_computation.7 | custom fusion | bytes 2629632 | tf_op jit(solution)/shard_map/gather | solution.py:20
  102.8 8.9 %add_convert_fusion = bf16[2048,320]{1,0:T(8,128)(2,1)S(1)} fusion(bf16[2048,320]{1,0:T(8,128)(2,1)} %gather_fusion.7, bf16[2048,320]{1,0:T(8,128)(2,1)} %gather_fusion.6, bf16[2048,320]{1,0:T(8,128)(2,1)} %gather_fusion.5, bf16[2048,320]{1,0:T(8,128)(2,1)} %gather_fusion.4, bf16[2048,320]{1,0:T(8,128)(2,1)} %gather_fusion.3, ...), kind=kLoop, calls=%fused_computation.19 | loop fusion | flops 17694720 | bytes 13131776 | tf_op jit(solution)/shard_map/convert_element_type | solution.py:50
  111.8 2.0 fusion.40
  113.8 0.0 reduce-scatter.3.cloned.1.call-update
  113.8 0.0 all-gather.5.cloned.1.call-start
  113.9 220.8 %reduce-scatter.3.cloned.1.call-done = f32[64,256]{1,0:T(8,128)} async-done(((f32[2048,256]{1,0:T(8,128)}), f32[64,256]{1,0:T(8,128)}) %reduce-scatter.3.cloned.1.call-update) | async-done | bytes 65552 | tf_op jit(solution)/shard_map/reduce_scatter | solution.py:52
  334.7 1.5 multiply_convert_fusion.3
  336.2 0.0 all-gather.5.cloned.1.call-update
  336.2 0.2 reduce-scatter.5.cloned.1.call-start
  336.6 0.1 fusion.28
  336.6 75.6 %all-gather.5.cloned.1.call-done = bf16[2048,256]{1,0:T(8,128)(2,1)} async-done(((bf16[64,256]{1,0:T(8,128)(2,1)}), bf16[2048,256]{1,0:T(8,128)(2,1)}) %all-gather.5.cloned.1.call-update) | async-done | bytes 1048592 | tf_op jit(solution)/shard_map/all_gather | solution.py:54
  412.2 3.6 gather_fusion.8
  415.9 0.0 collective-permute-start
  415.9 0.1 copy.31
  416.0 0.1 select_n.163
  416.1 0.1 reshape.203
  416.2 1.1 constant_dynamic-update-slice_fusion.1
  417.3 5.8 collective-permute-done
  423.1 0.7 constant_dynamic-update-slice_fusion
  423.8 2.1 gather_fusion.10
  426.0 0.0 copy-start.6
  426.0 0.0 copy-start.11
  426.0 2.2 gather_fusion.11
  428.2 2.1 gather_fusion.12
  430.3 2.1 gather_fusion.13
  432.5 2.1 gather_fusion.14
  434.6 2.1 gather_fusion.15
  436.8 2.1 gather_fusion.9
  438.9 2.1 gather_fusion.16
  441.1 0.3 fusion.16
  441.4 0.5 fusion.3
  441.9 5.1 scatter_custom_fusion
  447.0 1.1 slice.132
  448.0 0.0 collective-permute-start.1
  448.1 3.1 slice.112
  451.2 0.8 collective-permute-done.1
  451.9 6.0 scatter_custom_fusion.1
  457.9 2.7 convert_element_type.125
  460.6 0.0 reduce-scatter.5.cloned.1.call-update
  460.7 0.0 all-gather.7.cloned.1.call-start
  460.7 215.0 %reduce-scatter.5.cloned.1.call-done = bf16[64,256]{1,0:T(8,128)(2,1)} async-done(((bf16[2048,256]{1,0:T(8,128)(2,1)}), bf16[64,256]{1,0:T(8,128)(2,1)}) %reduce-scatter.5.cloned.1.call-update) | async-done | bytes 32784 | tf_op jit(solution)/shard_map/reduce_scatter | solution.py:78
  675.8 1.4 multiply_convert_fusion.2
  677.2 0.0 all-gather.7.cloned.1.call-update
  677.2 0.0 all-gather.9.cloned.1.call-start
  677.2 75.9 %all-gather.7.cloned.1.call-done = bf16[2048,256]{1,0:T(8,128)(2,1)} async-done(((bf16[64,256]{1,0:T(8,128)(2,1)}), bf16[2048,256]{1,0:T(8,128)(2,1)}) %all-gather.7.cloned.1.call-update) | async-done | bytes 1048592 | tf_op jit(solution)/shard_map/all_gather | solution.py:84
  753.1 2.5 fusion.41
  755.7 0.0 all-gather.9.cloned.1.call-update
  755.7 0.8 fusion.4
  756.6 26.4 %all-gather.9.cloned.1.call-done = f32[2560,256]{1,0:T(8,128)} async-done(((f32[320,256]{1,0:T(8,128)}), f32[2560,256]{1,0:T(8,128)}) %all-gather.9.cloned.1.call-update) | async-done | bytes 2621456 | tf_op jit(solution)/shard_map/all_gather | solution.py:88
  783.0 2.7 reduce_sum.9
  (38 shorter events, 0.1 us)
Async XLA Ops:
  7.2 433.9 %copy-start = (bf16[256,1024]{1,0:T(8,128)(2,1)S(1)}, bf16[256,1024]{1,0:T(8,128)(2,1)}, u32[]{:S(2)}) copy-start(bf16[256,1024]{1,0:T(8,128)(2,1)} %param.19) | copy-start | bytes 1572868
  7.2 327.5 %reduce-scatter.3.cloned.1.call-start = ((), (), s32[]{:S(2)}) async-start(), calls=%async_computation.2 | async-start | bytes 2162688 | tf_op jit(solution)/shard_map/reduce_scatter | solution.py:52
  8.7 4.6 copy-start.5
  102.8 8.9 %copy-start.3 = (bf16[320,256]{1,0:T(8,128)(2,1)S(1)}, bf16[320,256]{1,0:T(8,128)(2,1)}, u32[]{:S(2)}) copy-start(bf16[320,256]{1,0:T(8,128)(2,1)} %param.14) | copy-start | bytes 491524
  113.8 220.9 %copy-start.8 = (f32[256]{0:T(256)S(1)}, f32[256]{0:T(256)}, u32[]{:S(2)}) copy-start(f32[256]{0:T(256)} %param.15) | copy-start | bytes 3076
  113.8 222.6 %copy-start.10 = (s32[512]{0:T(512)S(1)}, s32[512]{0:T(512)}, u32[]{:S(2)}) copy-start(s32[512]{0:T(512)} %param.16) | copy-start | bytes 6148
  113.8 222.7 %copy-start.7 = (s32[64,8]{0,1:T(8,128)S(1)}, s32[64,8]{0,1:T(8,128)}, u32[]{:S(2)}) copy-start(s32[64,8]{0,1:T(8,128)} %param.17) | copy-start | bytes 6148
  113.8 222.7 %copy-start.9 = (s32[64]{0:T(128)S(1)}, s32[64]{0:T(128)}, u32[]{:S(2)}) copy-start(s32[64]{0:T(128)} %param.18) | copy-start | bytes 772
  113.8 298.4 %all-gather.5.cloned.1.call-start = ((), (), s32[]{:S(2)}) async-start(), calls=%async_computation.3 | async-start | bytes 1081344 | tf_op jit(solution)/shard_map/all_gather | solution.py:54
  336.2 339.6 %reduce-scatter.5.cloned.1.call-start = ((), (), s32[]{:S(2)}) async-start(), calls=%async_computation.4 | async-start | bytes 1081344 | tf_op jit(solution)/shard_map/reduce_scatter | solution.py:78
  412.2 3.9 copy-start.1
  415.9 7.2 collective-permute-start
  417.3 23.8 %copy-start.4 = (bf16[64,256]{1,0:T(8,128)(2,1)S(1)}, bf16[64,256]{1,0:T(8,128)(2,1)}, u32[]{:S(2)}) copy-start(bf16[64,256]{1,0:T(8,128)(2,1)} %multiply_convert_fusion.3) | copy-start | bytes 98308
  426.0 15.4 %copy-start.6 = (bf16[64,256]{1,0:T(8,128)(2,1)S(1)}, bf16[64,256]{1,0:T(8,128)(2,1)}, u32[]{:S(2)}) copy-start(bf16[64,256]{1,0:T(8,128)(2,1)} %param.21) | copy-start | bytes 98308
  426.0 15.4 %copy-start.11 = (bf16[1024,256]{1,0:T(8,128)(2,1)S(1)}, bf16[1024,256]{1,0:T(8,128)(2,1)}, u32[]{:S(2)}) copy-start(bf16[1024,256]{1,0:T(8,128)(2,1)} %param.20) | copy-start | bytes 1572868
  448.0 3.9 collective-permute-start.1
  457.9 217.8 %copy-start.2 = (f32[64,256]{1,0:T(8,128)S(1)}, f32[64,256]{1,0:T(8,128)}, u32[]{:S(2)}) copy-start(f32[64,256]{1,0:T(8,128)} %reduce-scatter.3.cloned.1.call-done) | copy-start | bytes 196612
  460.7 292.5 %all-gather.7.cloned.1.call-start = ((), (), s32[]{:S(2)}) async-start(), calls=%async_computation.5 | async-start | bytes 1081344 | tf_op jit(solution)/shard_map/all_gather | solution.py:84
  677.2 105.8 %all-gather.9.cloned.1.call-start = ((), (), s32[]{:S(2)}) async-start(), calls=%async_computation.6 | async-start | bytes 2949120 | tf_op jit(solution)/shard_map/all_gather | solution.py:88
Sparse Core Ops, SparseCore 0:
  113.9 220.6 reduce-scatter.2
  337.8 74.3 all-gather.4
  460.8 214.9 reduce-scatter.4
  678.8 74.3 all-gather.6
  755.8 27.1 all-gather.8
